TPU v7x, 32 devices: a whole 2x2x4 slice. The times are simulated.
32 devices in a mesh: groups: 2 (over x), ctx: 16 (over z, y, core).
Axes of the slice: x: 2, y: 2, z: 4, core: 2. Of those that a mesh axis runs over, the one named last changes fastest.
Arguments:
- tokens: bfloat16 [32, 8192], P('groups', 'ctx'), parts along dimension 0, may hold values from -6 to 6
- attn_gain: float32 [8192], replicated, may hold values from 0.1 to 1.9
- mlp_gain: float32 [8192], replicated, may hold values from 0.1 to 1.9
- q_weight: bfloat16 [8192, 8192], P(None, 'ctx'), may hold values from -0.0625 to 0.0625
- k_weight: bfloat16 [8192, 1024], P('ctx'), may hold values from -0.5 to 0.5
- v_weight: bfloat16 [8192, 1024], P('ctx'), may hold values from -0.0625 to 0.0625
- o_weight: bfloat16 [8192, 8192], P(None, 'ctx'), may hold values from -0.0625 to 0.0625
- gate_weight: bfloat16 [8192, 16384], P(None, 'ctx'), may hold values from -0.0625 to 0.0625
- up_weight: bfloat16 [8192, 16384], P(None, 'ctx'), may hold values from -0.0625 to 0.0625
- down_weight: bfloat16 [16384, 8192], P('ctx'), may hold values from -0.046875 to 0.046875
- prefix_keys: bfloat16 [8192, 1024], P(('groups', 'ctx')), parts along dimension 0, may hold values from -400 to 400
- prefix_values: bfloat16 [8192, 1024], P(('groups', 'ctx')), parts along dimension 0, may hold values from -36 to 36
- suffix_keys: bfloat16 [256, 16, 1024], P(('groups', 'ctx')), parts along dimension 0, may hold values from -18 to 18
- suffix_values: bfloat16 [256, 16, 1024], P(('groups', 'ctx')), parts along dimension 0, may hold values from -18 to 18
- suffix_lengths: int32 [32], P('groups'), parts along dimension 0, may hold values from 1 to 128, as said below
- suffix_table: int32 [32, 8], P(('groups', 'ctx')), parts along dimension 0, may hold values from 0 to 7, as said below
Outputs:
- layer_out: bfloat16 [32, 8192], P('groups', 'ctx'), parts along dimension 0
There are 2 independent parts, one for each index of `groups`. A program takes and returns all parts, laid end to end along the dimension named above; an argument that names none is the same for every part. Nothing has to cross between parts.
Inputs may be any that keep to these rules, and one draw needn't show every extreme that they name: `suffix_lengths`: at most 128; some sample has exactly 128. `suffix_table`: in every aligned block of 1 row, the entries name each of 0 to 7 exactly once.
All inputs are finite; a program needn't handle non-finite values.
Results may differ from a plain program's by a relative error of at most 0.014.
The roundings to bfloat16 on the way count: a program that leaves them out, or rounds other values in their place, can miss the bound.
Values may be sent and summed in bfloat16 or wider, within the bound.
A program may use at most 128 MiB of HBM per device.

v0:
```python
import math

import jax
import jax.numpy as jnp
from jax import lax
from jax.sharding import PartitionSpec as P

HEADS = 64
KV_HEADS = 8
HEAD_DIM = 128


EPSILON = 1e-05
ROPE_BASE = 500000.0


def rotate(matrix, position, columns):
    pair_index = (columns % HEAD_DIM // 2).astype(jnp.float32)
    frequency = jnp.exp(pair_index * (-2.0 * math.log(ROPE_BASE) / HEAD_DIM))
    angles = position.astype(jnp.float32)[:, None] * frequency[None, :]
    cosine = jnp.cos(angles[:, 0::2])
    sine_part = jnp.sin(angles[:, 0::2])
    even_part = matrix[:, 0::2]
    odd_part = matrix[:, 1::2]
    rotated_even = even_part * cosine - odd_part * sine_part
    rotated_odd = even_part * sine_part + odd_part * cosine
    return jnp.stack([rotated_even, rotated_odd], axis=-1).reshape(matrix.shape)


def normalized_rows(shard_rows, gain_vector):
    self_index = lax.axis_index("ctx")
    feature_width = shard_rows.shape[1]
    gathered_raw = lax.all_gather(shard_rows, "ctx", axis=1, tiled=True)
    widened = gathered_raw.astype(jnp.float32)
    mean_square = jnp.mean(widened * widened, axis=1, keepdims=True)
    gathered = (widened * lax.rsqrt(mean_square + EPSILON) * gain_vector).astype(jnp.bfloat16)
    local_part = lax.dynamic_slice_in_dim(gathered, self_index * feature_width, feature_width, 1)
    return (gathered, local_part)


def body(
    tokens,
    attn_gain,
    mlp_gain,
    q_weight,
    k_weight,
    v_weight,
    o_weight,
    gate_weight,
    up_weight,
    down_weight,
    prefix_keys,
    prefix_values,
    suffix_keys,
    suffix_values,
    suffix_lengths,
    suffix_table,
):
    self_index = lax.axis_index("ctx")
    devices = lax.axis_size("ctx")
    samples = tokens.shape[0]
    own_rows = suffix_table.shape[0]
    group_size = HEADS // KV_HEADS
    score_scale = 1.0 / math.sqrt(HEAD_DIM)
    prefix_rows = prefix_keys.shape[0]
    row_start = self_index * own_rows
    position = prefix_rows * devices + suffix_lengths
    own_position = lax.dynamic_slice_in_dim(position, row_start, own_rows, 0)
    own_lengths = lax.dynamic_slice_in_dim(suffix_lengths, row_start, own_rows, 0)
    attn_normed, local_normed = normalized_rows(tokens, attn_gain)
    query_width = q_weight.shape[1]
    query_cols = self_index * query_width + jnp.arange(query_width, dtype=jnp.int32)
    query_part = rotate(
        jnp.dot(attn_normed, q_weight, preferred_element_type=jnp.float32), position, query_cols
    ).astype(jnp.bfloat16)
    queries = lax.all_gather(query_part, "ctx", axis=1, tiled=True)
    key_width = k_weight.shape[1]
    key_term = jnp.dot(local_normed, k_weight, preferred_element_type=jnp.float32)
    value_term = jnp.dot(local_normed, v_weight, preferred_element_type=jnp.float32)
    fresh = lax.psum_scatter(
        jnp.concatenate([key_term, value_term], axis=1), "ctx", scatter_dimension=0, tiled=True
    )
    fresh_keys = rotate(
        fresh[:, :key_width], own_position, jnp.arange(key_width, dtype=jnp.int32)
    ).astype(jnp.bfloat16)
    fresh_values = fresh[:, key_width:].astype(jnp.bfloat16)
    query_heads = queries.reshape(samples, KV_HEADS, group_size, HEAD_DIM)
    head_keys = prefix_keys.reshape(prefix_rows, KV_HEADS, HEAD_DIM)
    head_values = prefix_values.reshape(prefix_rows, KV_HEADS, HEAD_DIM)
    scores = (
        jnp.einsum("sngd,tnd->sngt", query_heads, head_keys, preferred_element_type=jnp.float32)
        * score_scale
    )
    local_peak = jnp.max(scores, axis=-1)
    peak_heads = lax.pmax(local_peak, "ctx")
    weights = jnp.exp(scores - peak_heads[..., None])
    partial_total = jnp.sum(weights, axis=-1).reshape(samples, HEADS)
    summed = jnp.einsum(
        "sngt,tnd->sngd",
        weights.astype(jnp.bfloat16),
        head_values,
        preferred_element_type=jnp.float32,
    ).reshape(samples, HEADS * HEAD_DIM)
    every_sum, every_total = lax.psum((summed, partial_total), "ctx")
    prefix_sum = lax.dynamic_slice_in_dim(every_sum, row_start, own_rows, 0)
    prefix_total = lax.dynamic_slice_in_dim(every_total, row_start, own_rows, 0)
    prefix_peak = lax.dynamic_slice_in_dim(
        peak_heads.reshape(samples, HEADS), row_start, own_rows, 0
    )
    prefix_sum = prefix_sum.reshape(own_rows, HEADS, HEAD_DIM)
    own_queries = lax.dynamic_slice_in_dim(query_heads, row_start, own_rows, 0)
    suffix_span = suffix_table.shape[1] * suffix_keys.shape[1]
    owned_keys = suffix_keys[suffix_table].reshape(own_rows, suffix_span, KV_HEADS, HEAD_DIM)
    owned_values = suffix_values[suffix_table].reshape(own_rows, suffix_span, KV_HEADS, HEAD_DIM)
    every_key = jnp.concatenate(
        [owned_keys, fresh_keys.reshape(own_rows, 1, KV_HEADS, HEAD_DIM)], axis=1
    )
    every_value = jnp.concatenate(
        [owned_values, fresh_values.reshape(own_rows, 1, KV_HEADS, HEAD_DIM)], axis=1
    )
    slot_index = jnp.arange(suffix_span + 1, dtype=jnp.int32)
    live_mask = (slot_index[None, :] < own_lengths[:, None]) | (slot_index[None, :] == suffix_span)
    suffix_scores = (
        jnp.einsum("sngd,sjnd->sngj", own_queries, every_key, preferred_element_type=jnp.float32)
        * score_scale
    )
    suffix_scores = jnp.where(live_mask[:, None, None, :], suffix_scores, -1e30)
    suffix_peak = jnp.max(suffix_scores, axis=-1)
    suffix_weights = jnp.exp(suffix_scores - suffix_peak[..., None])
    suffix_total = jnp.sum(suffix_weights, axis=-1).reshape(own_rows, HEADS)
    suffix_sum = jnp.einsum(
        "sngj,sjnd->sngd",
        suffix_weights.astype(jnp.bfloat16),
        every_value,
        preferred_element_type=jnp.float32,
    ).reshape(own_rows, HEADS, HEAD_DIM)
    suffix_peak = suffix_peak.reshape(own_rows, HEADS)
    peak_all = jnp.maximum(prefix_peak, suffix_peak)
    prefix_factor = jnp.exp(prefix_peak - peak_all)
    suffix_factor = jnp.exp(suffix_peak - peak_all)
    numerator = prefix_sum * prefix_factor[..., None] + suffix_sum * suffix_factor[..., None]
    denominator = prefix_total * prefix_factor + suffix_total * suffix_factor
    attention = (
        (numerator / denominator[..., None])
        .reshape(own_rows, HEADS * HEAD_DIM)
        .astype(jnp.bfloat16)
    )
    attended = jnp.dot(
        lax.all_gather(attention, "ctx", axis=0, tiled=True),
        o_weight,
        preferred_element_type=jnp.float32,
    )
    mixed_rows = (tokens.astype(jnp.float32) + attended).astype(jnp.bfloat16)
    mlp_normed = normalized_rows(mixed_rows, mlp_gain)[0]
    gate_proj = jnp.dot(mlp_normed, gate_weight, preferred_element_type=jnp.float32)
    up_proj = jnp.dot(mlp_normed, up_weight, preferred_element_type=jnp.float32)
    hidden = (jax.nn.silu(gate_proj) * up_proj).astype(jnp.bfloat16)
    partial_value = jnp.dot(hidden, down_weight, preferred_element_type=jnp.float32)
    shares = lax.psum_scatter(partial_value, "ctx", scatter_dimension=1, tiled=True)
    return (mixed_rows.astype(jnp.float32) + shares).astype(jnp.bfloat16)


def solution(mesh):
    placed = (
        P("groups", "ctx"),
        P(),
        P(),
        P(None, "ctx"),
        P("ctx", None),
        P("ctx", None),
        P(None, "ctx"),
        P(None, "ctx"),
        P(None, "ctx"),
        P("ctx", None),
        P(("groups", "ctx"), None),
        P(("groups", "ctx"), None),
        P(("groups", "ctx"), None, None),
        P(("groups", "ctx"), None, None),
        P("groups"),
        P(("groups", "ctx"), None),
    )
    return jax.shard_map(
        body, mesh=mesh, in_specs=placed, out_specs=P("groups", "ctx"), check_vma=False
    )
```

profile of v0, /device:TPU:0, one launch (start us, length us, event | category | flops | bytes accessed | tf_op | source)
XLA Modules:
  0.0 365.9 jit_solution(18179177284620579872)
XLA Ops:
  6.5 24.2 %all_gather.12 = bf16[16,8192]{1,0:T(8,128)(2,1)S(1)} all-gather(bf16[16,512]{1,0:T(8,128)(2,1)} %param.16), channel_id=1, replica_groups=mesh['groups'=2,'ctx'=16] {'ctx'}, dimensions={1}, use_global_device_ids=true | all-gather | bytes 278528 | tf_op jit(solution)/shard_map/all_gather | solution.py:33
  30.7 0.2 fusion.7
  30.9 0.9 fusion.9
  31.8 4.6 %fusion.70 = f32[16,512]{1,0:T(8,128)S(1)} fusion(bf16[16,8192]{1,0:T(8,128)(2,1)S(1)} %fusion.9, bf16[8192,512]{1,0:T(8,128)(2,1)} %param.19), kind=kOutput, calls=%fused_computation.119 | convolution fusion | flops 134217728 | bytes 8683520 | tf_op jit(solution)/shard_map/dot_general | solution.py:74
  36.4 0.6 slice.27
  37.0 0.6 slice.29
  37.7 0.5 broadcast_add_fusion
  38.2 0.1 broadcast_multiply_fusion
  38.2 0.6 slice.28
  38.9 0.1 fusion.66
  39.0 0.1 copy.66
  39.1 30.1 %all_gather.13 = bf16[16,8192]{0,1:T(8,128)(2,1)S(1)} all-gather(bf16[16,512]{0,1:T(8,128)(2,1)S(1)} %bitcast.91), channel_id=1, replica_groups=mesh['groups'=2,'ctx'=16] {'ctx'}, dimensions={1}, use_global_device_ids=true | all-gather | bytes 278528 | tf_op jit(solution)/shard_map/all_gather | solution.py:76
  69.2 1.5 copy.68
  70.6 1.1 copy.91
  71.8 2.3 fusion.68
  74.0 60.5 %pmax.7 = f32[16,8,8]{2,0,1:T(8,128)S(1)} all-reduce(f32[16,8,8]{2,0,1:T(8,128)S(1)} %get-tuple-element.20), channel_id=1, replica_groups=mesh['groups'=2,'ctx'=16] {'ctx'}, use_global_device_ids=true, to_apply=%region_2.3 | all-reduce | flops 1024 | bytes 8192 | tf_op jit(solution)/shard_map/pmax | solution.py:95
  134.6 1.1 copy.92
  135.7 1.6 convolution_bitcast_fusion
  137.4 1.1 copy.107
  138.5 0.2 fusion.39
  138.7 1.5 fusion.41
  140.2 0.6 pad_maximum_fusion
  141.0 2.0 constant_dynamic-slice_fusion.1
  143.0 1.2 dynamic_slice.23
  144.2 1.6 fusion.4
  145.9 0.1 copy.72
  145.9 1.3 dynamic_slice.26
  147.8 0.2 slice.32
  148.1 2.0 copy.90
  150.1 0.7 fusion.58
  150.7 1.5 gather_fusion
  152.4 1.5 gather_fusion.1
  154.0 0.1 copy.78
  154.1 0.1 copy.79
  154.1 30.1 %psum.15 = f32[16,64]{1,0:T(8,128)S(1)} all-reduce(f32[16,64]{1,0:T(8,128)S(1)} %copy.79), channel_id=1, replica_groups=mesh['groups'=2,'ctx'=16] {'ctx'}, use_global_device_ids=true, to_apply=%region_7.8 | all-reduce | flops 1024 | bytes 8192 | tf_op jit(solution)/shard_map/psum | solution.py:104
  184.2 0.1 constant_dynamic-slice_fusion.2
  184.3 0.1 copy.89
  184.4 0.6 dynamic-slice
  185.0 0.6 compare_or_fusion
  185.5 0.1 fusion.67
  185.6 44.7 %all-reduce.4.cloned.1.call-done = (f32[16,2048]{1,0:T(8,128)}, f32[16,8192]{1,0:T(8,128)}) async-done(((f32[16,2048]{1,0:T(8,128)}, f32[16,8192]{1,0:T(8,128)}), (f32[16,2048]{1,0:T(8,128)}, f32[16,8192]{1,0:T(8,128)})) %all-reduce.4.cloned.1.call-update) | async-done | bytes 655376
  230.3 1.4 constant_dynamic-slice_fusion.3
  231.7 0.2 slice.31
  232.0 0.2 slice.33
  232.2 0.2 copy.74
  232.4 0.2 convert_element_type.98
  232.6 1.5 fusion.45
  234.1 0.3 fusion.69
  234.4 0.1 reshape.308
  234.5 0.2 fusion.33
  234.7 0.1 reshape.314
  234.8 0.2 fusion.19
  235.0 0.1 mul.212
  235.1 0.1 mul.215
  235.2 0.1 div.51
  235.3 1.0 convert_bitcast_fusion
  236.3 21.7 %all-gather = bf16[16,1,8192]{2,1,0:T(2,128)(2,1)S(1)} all-gather(bf16[1,1,8192]{2,1,0:T(2,128)(2,1)S(1)} %convert_bitcast_fusion), channel_id=1, replica_groups=mesh['groups'=2,'ctx'=16] {'ctx'}, dimensions={0}, use_global_device_ids=true | all-gather | bytes 278528 | tf_op jit(solution)/shard_map/all_gather | solution.py:149
  258.0 4.6 %fusion.3 = bf16[16,512]{1,0:T(8,128)(2,1)S(1)} fusion(bf16[8192,512]{1,0:T(8,128)(2,1)} %param.22, bf16[16,1,8192]{2,1,0:T(2,128)(2,1)S(1)} %all-gather, bf16[16,512]{1,0:T(8,128)(2,1)S(1)} %copy-done.3), kind=kOutput, calls=%fused_computation.10 | convolution fusion | flops 134242304 | bytes 8683520 | tf_op jit(solution)/shard_map/dot_general | solution.py:148
  262.5 18.3 %all_gather.15 = bf16[16,8192]{1,0:T(8,128)(2,1)S(1)} all-gather(bf16[16,512]{1,0:T(8,128)(2,1)S(1)} %fusion.3), channel_id=1, replica_groups=mesh['groups'=2,'ctx'=16] {'ctx'}, dimensions={1}, use_global_device_ids=true | all-gather | bytes 278528 | tf_op jit(solution)/shard_map/all_gather | solution.py:33
  280.9 0.2 fusion.10
  281.1 8.2 %fusion.31 = f32[16,1024]{1,0:T(8,128)S(1)} fusion(bf16[8192,1024]{1,0:T(8,128)(2,1)} %param.23, bf16[16,8192]{1,0:T(8,128)(2,1)S(1)} %all_gather.15, f32[8192]{0:T(1024)S(1)} %copy-done.2, f32[16]{0:T(128)S(1)} %add_rsqrt_fusion), kind=kOutput, calls=%fused_computation.45 | convolution fusion | flops 268959744 | bytes 17137728 | tf_op jit(solution)/shard_map/dot_general | solution.py:155
  289.2 13.7 %fusion.6 = f32[16,8192]{1,0:T(8,128)} fusion(bf16[1024,8192]{1,0:T(8,128)(2,1)} %param.25, bf16[8192,1024]{1,0:T(8,128)(2,1)} %param.24, f32[16,1024]{1,0:T(8,128)S(1)} %fusion.31, bf16[16,8192]{1,0:T(8,128)(2,1)S(1)} %all_gather.15, f32[8192]{0:T(1024)S(1)} %copy-done.2, f32[16]{0:T(128)S(1)} %add_rsqrt_fusion), kind=kOutput, calls=%fused_computation.18 | convolution fusion | flops 537493504 | bytes 34439232 | tf_op jit(solution)/shard_map/dot_general | solution.py:158
  303.0 54.7 %reduce-scatter.2.cloned.1.call-done = f32[16,512]{1,0:T(8,128)} async-done(((f32[16,8192]{1,0:T(8,128)}), f32[16,512]{1,0:T(8,128)}) %reduce-scatter.2.cloned.1.call-update) | async-done | bytes 32784 | tf_op jit(solution)/shard_map/reduce_scatter | solution.py:159
  357.7 1.4 add_convert_fusion
  (31 shorter events, 0.4 us)
Async XLA Ops:
  6.5 132.0 %copy-start = (bf16[512,1024]{1,0:T(8,128)(2,1)S(1)}, bf16[512,1024]{1,0:T(8,128)(2,1)}, u32[]{:S(2)}) copy-start(bf16[512,1024]{1,0:T(8,128)(2,1)} %param.21) | copy-start | bytes 3145732
  6.5 31.1 %copy-start.4 = (s32[16]{0:T(128)S(1)}, s32[16]{0:T(128)}, u32[]{:S(2)}) copy-start(s32[16]{0:T(128)} %param.30) | copy-start | bytes 196
  6.5 223.8 %all-reduce.4.cloned.1.call-start = ((), (), s32[]{:S(2)}) async-start(), calls=%async_computation.2 | async-start | bytes 1310720
  36.4 221.6 %copy-start.3 = (bf16[16,512]{1,0:T(8,128)(2,1)S(1)}, bf16[16,512]{1,0:T(8,128)(2,1)}, u32[]{:S(2)}) copy-start(bf16[16,512]{1,0:T(8,128)(2,1)} %param.16) | copy-start | bytes 49156
  134.6 49.8 %copy-start.5 = (u32[32]{0:T(128)S(1)}, u32[32]{0:T(128)}, u32[]{:S(2)}) copy-start(u32[32]{0:T(128)} %constant.89) | copy-start | bytes 388
  134.6 146.5 %copy-start.2 = (f32[8192]{0:T(1024)S(1)}, f32[8192]{0:T(1024)}, u32[]{:S(2)}) copy-start(f32[8192]{0:T(1024)} %param.18) | copy-start | bytes 98308
  140.9 216.8 %reduce-scatter.2.cloned.1.call-start = ((), (), s32[]{:S(2)}) async-start(), calls=%async_computation.1 | async-start | bytes 557056 | tf_op jit(solution)/shard_map/reduce_scatter | solution.py:159
  281.1 78.0 %copy-start.1 = (bf16[512,1024]{1,0:T(8,128)(2,1)S(1)}, bf16[512,1024]{1,0:T(8,128)(2,1)}, u32[]{:S(2)}) copy-start(bf16[512,1024]{1,0:T(8,128)(2,1)} %param.21) | copy-start | bytes 3145732
Sparse Core Ops, SparseCore 0:
  141.0 89.2 all-reduce.3
  303.1 54.5 reduce-scatter.1
where the time goes:
time: 367 us; the launch traced here: 366 us
  blocking collectives  185 us (50%)
  waiting for transfers between devices  99.5 us (27%)
  matrix products  37.2 us (10%)
  local copies, waits for them, and re-layouts  22 us (6%)
  between operations  14.3 us (4%)
  other arithmetic  8.09 us (2%)
    pmax x1, blocking collectives, body(): peak_heads = lax.pmax(local_peak, 'ctx')  60.5 us
    reduce_scatter x1, waiting for transfers between devices, body(): lax.psum_scatter(partial_value, 'ctx', scatter_dimension=1, tiled=True)  54.7 us
    unnamed x3, waiting for transfers between devices  44.7 us
    all_gather x2, blocking collectives, normalized_rows(): gathered_raw = lax.all_gather(shard_rows, 'ctx', axis=1, tiled=True)  42.5 us
    psum x1, blocking collectives, body(): every_sum, every_total = lax.psum((summed, partial_total), 'ctx')  30.1 us
    all_gather x1, blocking collectives, body(): queries = lax.all_gather(query_part, 'ctx', axis=1, tiled=True)  30.1 us
    all_gather x1, blocking collectives, body(): lax.all_gather(attention, 'ctx', axis=0, tiled=True)  21.7 us
    dot_general x1, matrix products, body(): jnp.dot(hidden, down_weight, preferred_element_type=jnp.float32)  13.7 us
  transfers between devices with their start and end apart: 2, of which 2 were waited for; matrix products, arithmetic and copies ran while one was open for 4% of the time, Pallas kernels for 0%

commit v1 on v0

--- a/solution.py
+++ b/solution.py
@@ -1,8 +1,11 @@
+import functools
 import math
 
 import jax
 import jax.numpy as jnp
 from jax import lax
+from jax.experimental import pallas as pl
+from jax.experimental.pallas import tpu as pltpu
 from jax.sharding import PartitionSpec as P
 
 HEADS = 64
@@ -38,7 +41,7 @@
     return (gathered, local_part)
 
 
-def body(
+def plain_body(
     tokens,
     attn_gain,
     mlp_gain,
@@ -160,6 +163,543 @@
     return (mixed_rows.astype(jnp.float32) + shares).astype(jnp.bfloat16)
 
 
+TOK, QRY, FRESH, PART, STAT, ATT, MIX, DOWN, PHASES = range(9)
+LANES = HEAD_DIM
+GROUP = HEADS // KV_HEADS
+FITS = 16
+
+
+def regroup(rows, inner, outer):
+    row = lax.broadcasted_iota(jnp.int32, (rows, rows), 0)
+    column = lax.broadcasted_iota(jnp.int32, (rows, rows), 1)
+    picked = (row % outer) * inner + row // outer
+    return jnp.where(column == picked, 1.0, 0.0).astype(jnp.bfloat16)
+
+
+def turn(block, cosine, signed_sine, even):
+    swapped = jnp.where(even, pltpu.roll(block, LANES - 1, 1), pltpu.roll(block, 1, 1))
+    return block * cosine + swapped * signed_sine
+
+
+def layer_kernel(
+    n,
+    prefix_tokens,
+    tokens,
+    attn_gain,
+    mlp_gain,
+    q_hbm,
+    k_hbm,
+    v_hbm,
+    o_hbm,
+    gate_hbm,
+    up_hbm,
+    down_hbm,
+    pk_hbm,
+    pv_hbm,
+    sk_hbm,
+    sv_hbm,
+    lengths,
+    table,
+    out,
+    qw,
+    kw,
+    vw,
+    ow,
+    gw,
+    uw,
+    dw,
+    pk,
+    pv,
+    sk,
+    sv,
+    again,
+    mgain,
+    tokbuf,
+    qbuf,
+    qperm,
+    psend,
+    precv,
+    ssend,
+    srecv,
+    fsend,
+    frecv,
+    attbuf,
+    attl,
+    mixbuf,
+    dsend,
+    drecv,
+    load_sem,
+    big_sem,
+    send_sem,
+    recv_sem,
+):
+    me = lax.axis_index("ctx")
+    partner = me + 1 - 2 * (me % 2)
+    half = n // 2
+    samples, width = tokens.shape
+    ffn = gw.shape[1]
+    scale = 1.0 / math.sqrt(HEAD_DIM)
+    f32, bf16 = jnp.float32, jnp.bfloat16
+
+    def load(source, target, index):
+        return pltpu.make_async_copy(source, target, load_sem.at[index])
+
+    def rows_of(d):
+        return pl.ds(pl.multiple_of(d * width, width), width)
+
+    def chunk(kind, d):
+        if kind == 0:
+            return pltpu.make_async_copy(q_hbm.at[rows_of(d)], qw.at[rows_of(d)], big_sem.at[0, d])
+        if kind == 1:
+            return pltpu.make_async_copy(o_hbm.at[rows_of(d)], ow.at[rows_of(d)], big_sem.at[1, d])
+        if kind == 2:
+            return pltpu.make_async_copy(
+                gate_hbm.at[rows_of(d)], gw.at[rows_of(d)], big_sem.at[2, d]
+            )
+        return pltpu.make_async_copy(up_hbm.at[rows_of(d)], uw.at[rows_of(d)], big_sem.at[3, d])
+
+    def down_chunk(step, target, place):
+        d = (me + 1 + step) % n
+        return pltpu.make_async_copy(
+            down_hbm.at[:, rows_of(d)],
+            target.at[pl.ds(pl.multiple_of(place * ffn, ffn), ffn)],
+            big_sem.at[4, step],
+        )
+
+    def remote(phase, source, target, slot, landed, device):
+        return pltpu.make_async_remote_copy(
+            src_ref=source,
+            dst_ref=target,
+            send_sem=send_sem.at[phase, slot],
+            recv_sem=recv_sem.at[phase, landed],
+            device_id={"ctx": device},
+            device_id_type=pl.DeviceIdType.MESH,
+        )
+
+    def loop(low, high, step):
+        def wrapped(index, carry):
+            step(index)
+            return carry
+
+        lax.fori_loop(low, high, wrapped, 0)
+
+    def spread(phase, buf):
+        loop(
+            1,
+            half,
+            lambda k: remote(
+                phase, buf.at[me], buf.at[me], k, me, (me + 2 * k) % n
+            ).start(),
+        )
+        remote(phase, buf.at[me], buf.at[me], 0, me, partner).start()
+
+    def collect(phase, buf):
+        def relay(k):
+            origin = (me + n - 2 * k) % n
+            remote(phase, buf.at[origin], buf.at[origin], 0, origin, partner).wait_recv()
+            remote(phase, buf.at[origin], buf.at[origin], half + k, origin, partner).start()
+
+        def arrive(k):
+            origin = (partner + n - 2 * k) % n
+            remote(phase, buf.at[origin], buf.at[origin], 0, origin, partner).wait_recv()
+
+        loop(1, half, relay)
+        loop(0, half, arrive)
+
+    def drain(phase, buf):
+        def one(k):
+            remote(phase, buf.at[me], buf.at[me], k, me, partner).wait_send()
+
+        loop(0, half, one)
+        loop(half + 1, n, one)
+
+    def scatter_one(phase, source, target, k):
+        device = (me + k) % n
+        remote(phase, source.at[device], target.at[me], k, me, device).start()
+
+    def gather_one(phase, source, target, k):
+        origin = (me + n - k) % n
+        remote(phase, source.at[origin], target.at[origin], k, origin, origin).wait_recv()
+
+    def sent_one(phase, source, target, k):
+        device = (me + k) % n
+        remote(phase, source.at[device], target.at[me], k, me, device).wait_send()
+
+    first = load(tokens, tokbuf.at[me], 0)
+    first.start()
+    small = [
+        load(attn_gain, again, 1),
+        load(mlp_gain, mgain, 2),
+        load(k_hbm, kw, 3),
+        load(v_hbm, vw, 4),
+        load(pk_hbm, pk, 5),
+        load(pv_hbm, pv, 6),
+        load(sk_hbm, sk, 7),
+        load(sv_hbm, sv, 8),
+    ]
+    barrier = pltpu.get_barrier_semaphore()
+    loop(
+        1,
+        n,
+        lambda k: pl.semaphore_signal(
+            barrier,
+            inc=1,
+            device_id={"ctx": (me + k) % n},
+            device_id_type=pl.DeviceIdType.MESH,
+        ),
+    )
+    small[0].start()
+    loop(0, n, lambda d: chunk(0, d).start())
+    for copy in small[1:]:
+        copy.start()
+    first.wait()
+    pl.semaphore_wait(barrier, n - 1)
+    spread(TOK, tokbuf)
+    loop(0, n, lambda d: chunk(1, d).start())
+
+    def start_pair(d):
+        chunk(2, d).start()
+        chunk(3, d).start()
+
+    loop(0, n, start_pair)
+    loop(0, half, lambda i: down_chunk(i, dw, i).start())
+
+    lane = lax.broadcasted_iota(jnp.int32, (samples, LANES), 1)
+    row = lax.broadcasted_iota(jnp.int32, (samples, LANES), 0)
+    even = lane % 2 == 0
+    pair_index = (lane // 2).astype(f32)
+    frequency = jnp.exp(pair_index * (-2.0 * math.log(ROPE_BASE) / HEAD_DIM))
+    position = jnp.zeros((samples, LANES), jnp.int32)
+    for s in range(samples):
+        position = jnp.where(row == s, lengths[s] + prefix_tokens, position)
+    angles = position.astype(f32) * frequency
+    cosine = jnp.cos(angles)
+    sine = jnp.where(even, -1.0, 1.0) * jnp.sin(angles)
+    own_length = lengths[me]
+    own_angles = (own_length + prefix_tokens).astype(f32) * frequency
+    own_cosine = jnp.cos(own_angles)[:KV_HEADS]
+    own_sine = (jnp.where(even, -1.0, 1.0) * jnp.sin(own_angles))[:KV_HEADS]
+    to_sample = regroup(samples * GROUP, samples, GROUP)
+    square = regroup(samples * samples, samples, samples)
+
+    def inverse_root(buf):
+        def add(d, total):
+            block = buf[d].astype(f32)
+            return total + jnp.sum(block * block, axis=1, keepdims=True)
+
+        total = lax.fori_loop(0, n, add, jnp.zeros((samples, 1), f32))
+        return lax.rsqrt(total / (n * width) + EPSILON)
+
+    def normed(buf, root, gain, d):
+        return (buf[d].astype(f32) * root * gain[:, rows_of(d)]).astype(bf16)
+
+    for copy in small[:2]:
+        copy.wait()
+    collect(TOK, tokbuf)
+    root = inverse_root(tokbuf)
+
+    def q_step(d, total):
+        chunk(0, d).wait()
+        return total + jnp.dot(
+            normed(tokbuf, root, again, d), qw[rows_of(d), :], preferred_element_type=f32
+        )
+
+    query = lax.fori_loop(0, n, q_step, jnp.zeros((samples, width), f32))
+    for j in range(width // LANES):
+        piece = slice(j * LANES, (j + 1) * LANES)
+        qbuf[me, :, piece] = turn(query[:, piece], cosine, sine, even).astype(bf16)
+    spread(QRY, qbuf)
+    loop(half, n, lambda i: down_chunk(i, qw, i - half).start())
+
+    for copy in small[2:]:
+        copy.wait()
+    mine = normed(tokbuf, root, again, me)
+    terms = [
+        jnp.dot(mine, kw[...], preferred_element_type=f32),
+        jnp.dot(mine, vw[...], preferred_element_type=f32),
+    ]
+    stacked = jnp.concatenate(
+        [
+            term[:, c * LANES : (c + 1) * LANES]
+            for term in terms
+            for c in range(KV_HEADS)
+        ],
+        axis=0,
+    )
+    upper = stacked.astype(bf16)
+    lower = (stacked - upper.astype(f32)).astype(bf16)
+    by_owner = jnp.dot(square, upper, preferred_element_type=f32) + jnp.dot(
+        square, lower, preferred_element_type=f32
+    )
+    by_owner = by_owner.reshape(n, 2 * KV_HEADS, LANES)
+    fsend[...] = by_owner
+    loop(1, n, lambda k: scatter_one(FRESH, fsend, frecv, k))
+    frecv[me] = fsend[me]
+
+    collect(QRY, qbuf)
+    stat_lane = lax.broadcasted_iota(jnp.int32, (samples * GROUP, LANES), 1)
+    stats = jnp.zeros((samples * GROUP, LANES), f32)
+    per_device = width // LANES
+    held = []
+    for k in range(KV_HEADS):
+        piece = slice(k * LANES, (k + 1) * LANES)
+        heads = [k * GROUP + g for g in range(GROUP)]
+        raw = jnp.concatenate(
+            [
+                qbuf[h // per_device, :, (h % per_device) * LANES : (h % per_device + 1) * LANES]
+                for h in heads
+            ],
+            axis=0,
+        )
+        arranged = jnp.dot(to_sample, raw, preferred_element_type=f32)
+        qperm[k] = arranged
+        scores = (
+            lax.dot_general(
+                arranged.astype(bf16),
+                pk[:, piece],
+                (((1,), (1,)), ((), ())),
+                preferred_element_type=f32,
+            )
+            * scale
+        )
+        peak = jnp.max(scores, axis=1, keepdims=True)
+        weights = jnp.exp(scores - peak)
+        total = jnp.sum(weights, axis=1, keepdims=True)
+        summed = jnp.dot(weights.astype(bf16), pv[:, piece], preferred_element_type=f32)
+        stats = jnp.where(stat_lane == k, peak, stats)
+        stats = jnp.where(stat_lane == k + LANES // 2, total, stats)
+        held.append(summed.reshape(samples, GROUP, LANES))
+        if k % 2 == 1:
+            psend[:, (k - 1) * GROUP : (k + 1) * GROUP, :] = jnp.concatenate(
+                held, axis=1
+            ).astype(bf16)
+            held = []
+    ssend[...] = stats.reshape(samples, GROUP, LANES)
+
+    def send_part(k):
+        scatter_one(STAT, ssend, srecv, k)
+        scatter_one(PART, psend, precv, k)
+
+    loop(1, n, send_part)
+    srecv[me] = ssend[me]
+    precv[me] = psend[me]
+
+    loop(1, n, lambda k: gather_one(FRESH, fsend, frecv, k))
+    fresh = lax.fori_loop(
+        0, n, lambda d, total: total + frecv[d], jnp.zeros((2 * KV_HEADS, LANES), f32)
+    )
+    fresh_keys = (
+        turn(fresh[:KV_HEADS], own_cosine, own_sine, even[:KV_HEADS]).astype(bf16).astype(f32)
+    )
+    fresh_values = fresh[KV_HEADS:].astype(bf16).astype(f32)
+    blocks, block = sk.shape[0], sk.shape[1]
+    span = blocks * block
+    place = lax.broadcasted_iota(jnp.int32, (GROUP, span), 1)
+    slot = jnp.zeros((GROUP, span), jnp.int32)
+    for i in range(blocks):
+        slot = jnp.where(place // block == table[0, i], i * block + place % block, slot)
+    live = slot < own_length
+    own_lane = lax.broadcasted_iota(jnp.int32, (GROUP, LANES), 1)
+    own_peaks = jnp.zeros((GROUP, LANES), f32)
+    own_totals = jnp.zeros((GROUP, LANES), f32)
+    own_sums = []
+    for k in range(KV_HEADS):
+        piece = slice(k * LANES, (k + 1) * LANES)
+        mine_q = qperm[k, pl.ds(pl.multiple_of(me * GROUP, GROUP), GROUP), :]
+        scores = (
+            lax.dot_general(
+                mine_q.astype(bf16),
+                sk[:, :, piece].reshape(span, LANES),
+                (((1,), (1,)), ((), ())),
+                preferred_element_type=f32,
+            )
+            * scale
+        )
+        scores = jnp.where(live, scores, -1e30)
+        fresh_score = (
+            jnp.sum(mine_q * fresh_keys[k : k + 1], axis=1, keepdims=True) * scale
+        )
+        peak = jnp.maximum(jnp.max(scores, axis=1, keepdims=True), fresh_score)
+        weights = jnp.where(live, jnp.exp(scores - peak), 0.0)
+        fresh_weight = jnp.exp(fresh_score - peak)
+        total = jnp.sum(weights, axis=1, keepdims=True) + fresh_weight
+        summed = jnp.dot(
+            weights.astype(bf16),
+            sv[:, :, piece].reshape(span, LANES),
+            preferred_element_type=f32,
+        )
+        own_sums.append(
+            summed + fresh_weight.astype(bf16).astype(f32) * fresh_values[k : k + 1]
+        )
+        own_peaks = jnp.where(own_lane == k, peak, own_peaks)
+        own_totals = jnp.where(own_lane == k, total, own_totals)
+
+    loop(1, n, lambda k: gather_one(STAT, ssend, srecv, k))
+    head_lane = own_lane < KV_HEADS
+    best = lax.fori_loop(0, n, lambda d, top: jnp.maximum(top, srecv[d]), own_peaks)
+    own_factor = jnp.exp(own_peaks - best)
+    loop(1, n, lambda k: gather_one(PART, psend, precv, k))
+
+    def column(tile):
+        return jnp.concatenate(
+            [
+                jnp.broadcast_to(tile[:, k : k + 1], (GROUP, LANES))
+                for k in range(KV_HEADS)
+            ],
+            axis=0,
+        )
+
+    def merge(d, carry):
+        numerator, denominator = carry
+        stat = srecv[d]
+        factor = jnp.where(head_lane, jnp.exp(jnp.minimum(stat - best, 0.0)), 0.0)
+        denominator = denominator + factor * pltpu.roll(stat, LANES // 2, 1)
+        return numerator + column(factor) * precv[d].astype(f32), denominator
+
+    numerator, denominator = lax.fori_loop(
+        0,
+        n,
+        merge,
+        (column(own_factor) * jnp.concatenate(own_sums, axis=0), own_factor * own_totals),
+    )
+    denominator = jnp.where(head_lane, denominator, 1.0)
+    attbuf[me] = (numerator / column(denominator)).astype(bf16)
+    spread(ATT, attbuf)
+    collect(ATT, attbuf)
+    for j in range(HEADS // samples):
+        rows = attbuf[:, j * samples : (j + 1) * samples, :].reshape(samples * samples, LANES)
+        swapped = jnp.dot(square, rows, preferred_element_type=f32).astype(bf16)
+        for i in range(samples):
+            h = j * samples + i
+            attl[
+                h // per_device, :, (h % per_device) * LANES : (h % per_device + 1) * LANES
+            ] = swapped[i * samples : (i + 1) * samples]
+
+    def o_step(d, total):
+        chunk(1, d).wait()
+        return total + jnp.dot(attl[d], ow[rows_of(d), :], preferred_element_type=f32)
+
+    attended = lax.fori_loop(0, n, o_step, jnp.zeros((samples, width), f32))
+    mixbuf[me] = (tokbuf[me].astype(f32) + attended).astype(bf16)
+    spread(MIX, mixbuf)
+    collect(MIX, mixbuf)
+    root = inverse_root(mixbuf)
+
+    def ffn_step(d, carry):
+        gate, up = carry
+        chunk(2, d).wait()
+        chunk(3, d).wait()
+        part = normed(mixbuf, root, mgain, d)
+        gate = gate + jnp.dot(part, gw[rows_of(d), :], preferred_element_type=f32)
+        up = up + jnp.dot(part, uw[rows_of(d), :], preferred_element_type=f32)
+        return gate, up
+
+    zero = jnp.zeros((samples, ffn), f32)
+    gate, up = lax.fori_loop(0, n, ffn_step, (zero, zero))
+    hidden = (gate / (1.0 + jnp.exp(-gate)) * up).astype(bf16)
+
+    def down_step(step, weights, place):
+        down_chunk(step, weights, place).wait()
+        term = jnp.dot(
+            hidden,
+            weights[pl.ds(pl.multiple_of(place * ffn, ffn), ffn), :],
+            preferred_element_type=f32,
+        )
+        return term
+
+    def down_low(i):
+        dsend[(me + 1 + i) % n] = down_step(i, dw, i).astype(bf16)
+        scatter_one(DOWN, dsend, drecv, i + 1)
+
+    def down_high(i):
+        dsend[(me + 1 + i) % n] = down_step(i, qw, i - half).astype(bf16)
+        scatter_one(DOWN, dsend, drecv, i + 1)
+
+    loop(0, half, down_low)
+    loop(half, n - 1, down_high)
+    total = mixbuf[me].astype(f32) + down_step(n - 1, qw, half - 1)
+
+    for phase, buf in ((TOK, tokbuf), (QRY, qbuf), (ATT, attbuf), (MIX, mixbuf)):
+        drain(phase, buf)
+    for phase, source, target in (
+        (FRESH, fsend, frecv),
+        (STAT, ssend, srecv),
+        (PART, psend, precv),
+    ):
+        loop(1, n, functools.partial(sent_one, phase, source, target))
+
+    def finish(k, total):
+        gather_one(DOWN, dsend, drecv, k)
+        return total + drecv[(me + n - k) % n].astype(f32)
+
+    total = lax.fori_loop(1, n, finish, total)
+    out[...] = total.astype(bf16)
+    loop(1, n, functools.partial(sent_one, DOWN, dsend, drecv))
+
+
+def body(*args):
+    tokens, q_weight, gate_weight = args[0], args[3], args[7]
+    prefix_keys, suffix_keys, suffix_table = args[10], args[12], args[15]
+    n = lax.axis_size("ctx")
+    samples, width = tokens.shape
+    ffn = gate_weight.shape[1]
+    fits = (
+        samples == n == FITS == 2 * KV_HEADS
+        and suffix_table.shape[0] == 1
+        and width % LANES == 0
+        and n * width == HEADS * HEAD_DIM
+        and q_weight.shape[0] == (n // 2) * ffn
+        and suffix_keys.shape[0] * suffix_keys.shape[1] == LANES
+    )
+    if not fits:
+        return plain_body(*args)
+    args = list(args)
+    args[1] = args[1].reshape(1, -1)
+    args[2] = args[2].reshape(1, -1)
+    bf16, f32 = jnp.bfloat16, jnp.float32
+    kept = [args[i] for i in (3, 4, 5, 6, 7, 8)]
+    exchange = pltpu.VMEM((n, samples, width), bf16)
+    parts = pltpu.VMEM((n, HEADS, LANES), bf16)
+    stats = pltpu.VMEM((n, GROUP, LANES), f32)
+    fresh = pltpu.VMEM((n, 2 * KV_HEADS, LANES), f32)
+    anywhere = pl.BlockSpec(memory_space=pl.ANY)
+    scalars = pl.BlockSpec(memory_space=pltpu.SMEM)
+    return pl.pallas_call(
+        functools.partial(layer_kernel, n, prefix_keys.shape[0] * n),
+        out_shape=jax.ShapeDtypeStruct((samples, width), bf16),
+        in_specs=[anywhere] * 14 + [scalars] * 2,
+        out_specs=pl.BlockSpec(memory_space=pltpu.VMEM),
+        scratch_shapes=[pltpu.VMEM(w.shape, bf16) for w in kept]
+        + [pltpu.VMEM(((n // 2) * ffn, width), bf16)]
+        + [pltpu.VMEM(args[i].shape, bf16) for i in (10, 11, 12, 13)]
+        + [pltpu.VMEM((1, n * width), f32)] * 2
+        + [
+            exchange,
+            exchange,
+            pltpu.VMEM((KV_HEADS, samples * GROUP, LANES), f32),
+            parts,
+            parts,
+            stats,
+            stats,
+            fresh,
+            fresh,
+            parts,
+            exchange,
+            exchange,
+            exchange,
+            exchange,
+            pltpu.SemaphoreType.DMA((9,)),
+            pltpu.SemaphoreType.DMA((5, n)),
+            pltpu.SemaphoreType.DMA((PHASES, n)),
+            pltpu.SemaphoreType.DMA((PHASES, n)),
+        ],
+        compiler_params=pltpu.CompilerParams(
+            collective_id=0, has_side_effects=True, vmem_limit_bytes=67043328
+        ),
+        name="layer",
+    )(*args)
+
+
 def solution(mesh):
     placed = (
         P("groups", "ctx"),

time: 367 us -> 70.2 us (0.19)
  blocking collectives: 185 us -> 0 us
  waiting for transfers between devices: 99.5 us -> 0 us
  Pallas kernels: 0 us -> 68.3 us
  matrix products: 37.2 us -> 0 us
  local copies, waits for them, and re-layouts: 22 us -> 1.32 us
  between operations: 14.3 us -> 0.01 us
  other arithmetic: 8.09 us -> 0 us
    all_gather x4 -> x0, blocking collectives: 94.2 us -> none  [the longest x2 42.5 us: normalized_rows(): gathered_raw = lax.all_gather(shard_rows, 'ctx', axis=1, tiled=True)]
    pallas_call x0 -> x1, Pallas kernels: none -> 68.3 us  [body(): pl.pallas_call(functools.partial(layer_kernel, n, prefix_keys.shape[0] *...]
    pmax x1 -> x0, blocking collectives: 60.5 us -> none  [body(): peak_heads = lax.pmax(local_peak, 'ctx')]
    reduce_scatter x1 -> x0, waiting for transfers between devices: 54.7 us -> none  [body(): lax.psum_scatter(partial_value, 'ctx', scatter_dimension=1, tiled=True)]
    unnamed x3 -> x0, waiting for transfers between devices: 44.7 us -> none
    dot_general x10 -> x0, matrix products: 37.2 us -> none  [the longest x1 13.7 us: body(): jnp.dot(hidden, down_weight, preferred_element_type=jnp.float32)]
    psum x1 -> x0, blocking collectives: 30.1 us -> none  [body(): every_sum, every_total = lax.psum((summed, partial_total), 'ctx')]
    unnamed x20 -> x1, local copies, waits for them, and re-layouts: 6.18 us -> 1.32 us
  transfers between devices with their start and end apart: 2 -> 0, of which waited for: 2 -> 0; matrix products, arithmetic and copies ran while one was open for 4% -> 0% of each run, Pallas kernels for 0% -> 0%
where the time goes in v1:
time: 70.2 us; the launch traced here: 69.6 us
  Pallas kernels  68.3 us (97%)
  local copies, waits for them, and re-layouts  1.32 us (2%)
    pallas_call x1, Pallas kernels, body(): pl.pallas_call(functools.partial(layer_kernel, n, prefix_keys.shape[0] *...  68.3 us

profile of v1, /device:TPU:0, one launch (start us, length us, event | category | flops | bytes accessed | tf_op | source)
XLA Modules:
  0.0 69.6 jit_solution(6385924401116096155)
XLA Ops:
  0.0 68.3 %layer.1 = bf16[16,512]{1,0:T(8,128)(2,1)} custom-call(bf16[16,512]{1,0:T(8,128)(2,1)} %tokens.1, f32[1,8192]{1,0:T(1,128)} %bitcast.2, f32[1,8192]{1,0:T(1,128)} %bitcast.3, bf16[8192,512]{1,0:T(8,128)(2,1)} %q_hbm.1, bf16[512,1024]{1,0:T(8,128)(2,1)} %k_hbm.1, bf16[512,1024]{1,0:T(8,128)(2,1)} %v_hbm.1, bf16[8192,512]{1,0:T(8,128)(2,1)} %o_hbm.1, ...), custom_call_target="tpu_custom_call" | custom-call | tf_op jit(solution)/shard_map/layer/pallas_call | solution.py:667
  68.3 1.3 %copy.18 = bf16[16,512]{1,0:T(8,128)(2,1)} copy(bf16[16,512]{1,0:T(8,128)(2,1)} %layer.1) | data formatting | bytes 32768

commit v2 on v1

--- a/solution.py
+++ b/solution.py
@@ -163,7 +163,7 @@
     return (mixed_rows.astype(jnp.float32) + shares).astype(jnp.bfloat16)
 
 
-TOK, QRY, FRESH, PART, STAT, ATT, MIX, DOWN, PHASES = range(9)
+TOK, QRY, FRESH, PART, STAT, ATT, MIX, PAIR, DOWN, PHASES = range(10)
 LANES = HEAD_DIM
 GROUP = HEADS // KV_HEADS
 FITS = 16
@@ -224,9 +224,9 @@
     fsend,
     frecv,
     attbuf,
-    attl,
     mixbuf,
     dsend,
+    dpair,
     drecv,
     load_sem,
     big_sem,
@@ -236,6 +236,8 @@
     me = lax.axis_index("ctx")
     partner = me + 1 - 2 * (me % 2)
     half = n // 2
+    core = me % 2
+    chip = me // 2
     samples, width = tokens.shape
     ffn = gw.shape[1]
     scale = 1.0 / math.sqrt(HEAD_DIM)
@@ -259,7 +261,7 @@
         return pltpu.make_async_copy(up_hbm.at[rows_of(d)], uw.at[rows_of(d)], big_sem.at[3, d])
 
     def down_chunk(step, target, place):
-        d = (me + 1 + step) % n
+        d = 2 * ((chip + 1 + step) % half) + (core + 1 + step // half) % 2
         return pltpu.make_async_copy(
             down_hbm.at[:, rows_of(d)],
             target.at[pl.ds(pl.multiple_of(place * ffn, ffn), ffn)],
@@ -387,7 +389,7 @@
             block = buf[d].astype(f32)
             return total + jnp.sum(block * block, axis=1, keepdims=True)
 
-        total = lax.fori_loop(0, n, add, jnp.zeros((samples, 1), f32))
+        total = lax.fori_loop(0, n, add, jnp.zeros((samples, 1), f32), unroll=True)
         return lax.rsqrt(total / (n * width) + EPSILON)
 
     def normed(buf, root, gain, d):
@@ -404,7 +406,7 @@
             normed(tokbuf, root, again, d), qw[rows_of(d), :], preferred_element_type=f32
         )
 
-    query = lax.fori_loop(0, n, q_step, jnp.zeros((samples, width), f32))
+    query = lax.fori_loop(0, n, q_step, jnp.zeros((samples, width), f32), unroll=4)
     for j in range(width // LANES):
         piece = slice(j * LANES, (j + 1) * LANES)
         qbuf[me, :, piece] = turn(query[:, piece], cosine, sine, even).astype(bf16)
@@ -433,10 +435,9 @@
     )
     by_owner = by_owner.reshape(n, 2 * KV_HEADS, LANES)
     fsend[...] = by_owner
+    collect(QRY, qbuf)
     loop(1, n, lambda k: scatter_one(FRESH, fsend, frecv, k))
     frecv[me] = fsend[me]
-
-    collect(QRY, qbuf)
     stat_lane = lax.broadcasted_iota(jnp.int32, (samples * GROUP, LANES), 1)
     stats = jnp.zeros((samples * GROUP, LANES), f32)
     per_device = width // LANES
@@ -452,7 +453,7 @@
             axis=0,
         )
         arranged = jnp.dot(to_sample, raw, preferred_element_type=f32)
-        qperm[k] = arranged
+        qperm[k] = arranged.astype(bf16).reshape(samples, GROUP, LANES)
         scores = (
             lax.dot_general(
                 arranged.astype(bf16),
@@ -486,7 +487,7 @@
 
     loop(1, n, lambda k: gather_one(FRESH, fsend, frecv, k))
     fresh = lax.fori_loop(
-        0, n, lambda d, total: total + frecv[d], jnp.zeros((2 * KV_HEADS, LANES), f32)
+        0, n, lambda d, total: total + frecv[d], jnp.zeros((2 * KV_HEADS, LANES), f32), unroll=True
     )
     fresh_keys = (
         turn(fresh[:KV_HEADS], own_cosine, own_sine, even[:KV_HEADS]).astype(bf16).astype(f32)
@@ -505,7 +506,7 @@
     own_sums = []
     for k in range(KV_HEADS):
         piece = slice(k * LANES, (k + 1) * LANES)
-        mine_q = qperm[k, pl.ds(pl.multiple_of(me * GROUP, GROUP), GROUP), :]
+        mine_q = qperm[k, me].astype(f32)
         scores = (
             lax.dot_general(
                 mine_q.astype(bf16),
@@ -536,7 +537,7 @@
 
     loop(1, n, lambda k: gather_one(STAT, ssend, srecv, k))
     head_lane = own_lane < KV_HEADS
-    best = lax.fori_loop(0, n, lambda d, top: jnp.maximum(top, srecv[d]), own_peaks)
+    best = lax.fori_loop(0, n, lambda d, top: jnp.maximum(top, srecv[d]), own_peaks, unroll=True)
     own_factor = jnp.exp(own_peaks - best)
     loop(1, n, lambda k: gather_one(PART, psend, precv, k))
 
@@ -561,25 +562,27 @@
         n,
         merge,
         (column(own_factor) * jnp.concatenate(own_sums, axis=0), own_factor * own_totals),
+        unroll=2,
     )
     denominator = jnp.where(head_lane, denominator, 1.0)
     attbuf[me] = (numerator / column(denominator)).astype(bf16)
     spread(ATT, attbuf)
+    drain(QRY, qbuf)
     collect(ATT, attbuf)
     for j in range(HEADS // samples):
         rows = attbuf[:, j * samples : (j + 1) * samples, :].reshape(samples * samples, LANES)
         swapped = jnp.dot(square, rows, preferred_element_type=f32).astype(bf16)
         for i in range(samples):
             h = j * samples + i
-            attl[
+            qbuf[
                 h // per_device, :, (h % per_device) * LANES : (h % per_device + 1) * LANES
             ] = swapped[i * samples : (i + 1) * samples]
 
     def o_step(d, total):
         chunk(1, d).wait()
-        return total + jnp.dot(attl[d], ow[rows_of(d), :], preferred_element_type=f32)
-
-    attended = lax.fori_loop(0, n, o_step, jnp.zeros((samples, width), f32))
+        return total + jnp.dot(qbuf[d], ow[rows_of(d), :], preferred_element_type=f32)
+
+    attended = lax.fori_loop(0, n, o_step, jnp.zeros((samples, width), f32), unroll=4)
     mixbuf[me] = (tokbuf[me].astype(f32) + attended).astype(bf16)
     spread(MIX, mixbuf)
     collect(MIX, mixbuf)
@@ -595,7 +598,7 @@
         return gate, up
 
     zero = jnp.zeros((samples, ffn), f32)
-    gate, up = lax.fori_loop(0, n, ffn_step, (zero, zero))
+    gate, up = lax.fori_loop(0, n, ffn_step, (zero, zero), unroll=4)
     hidden = (gate / (1.0 + jnp.exp(-gate)) * up).astype(bf16)
 
     def down_step(step, weights, place):
@@ -607,19 +610,35 @@
         )
         return term
 
-    def down_low(i):
-        dsend[(me + 1 + i) % n] = down_step(i, dw, i).astype(bf16)
-        scatter_one(DOWN, dsend, drecv, i + 1)
-
-    def down_high(i):
-        dsend[(me + 1 + i) % n] = down_step(i, qw, i - half).astype(bf16)
-        scatter_one(DOWN, dsend, drecv, i + 1)
-
-    loop(0, half, down_low)
-    loop(half, n - 1, down_high)
+    def to_pair(c, slot):
+        return remote(PAIR, dsend.at[c], dpair.at[c], slot, c, partner)
+
+    def down_low(i, carry):
+        c = (chip + 1 + i) % half
+        dsend[c] = down_step(i, dw, i).astype(bf16)
+        to_pair(c, i).start()
+        return carry
+
+    lax.fori_loop(0, half, down_low, 0, unroll=2)
+
+    def to_chip(k):
+        c = (chip + k) % half
+        return remote(DOWN, dpair.at[c], drecv.at[chip], k, chip, 2 * c + core)
+
+    def down_high(i, carry):
+        c = (chip + 1 + i) % half
+        term = down_step(half + i, qw, i)
+        to_pair(c, 0).wait_recv()
+        dpair[c] = (term + dpair[c].astype(f32)).astype(bf16)
+        to_chip(i + 1).start()
+        return carry
+
+    lax.fori_loop(0, half - 1, down_high, 0)
     total = mixbuf[me].astype(f32) + down_step(n - 1, qw, half - 1)
-
-    for phase, buf in ((TOK, tokbuf), (QRY, qbuf), (ATT, attbuf), (MIX, mixbuf)):
+    to_pair(chip, 0).wait_recv()
+    total = total + dpair[chip].astype(f32)
+
+    for phase, buf in ((TOK, tokbuf), (ATT, attbuf), (MIX, mixbuf)):
         drain(phase, buf)
     for phase, source, target in (
         (FRESH, fsend, frecv),
@@ -629,12 +648,16 @@
         loop(1, n, functools.partial(sent_one, phase, source, target))
 
     def finish(k, total):
-        gather_one(DOWN, dsend, drecv, k)
-        return total + drecv[(me + n - k) % n].astype(f32)
-
-    total = lax.fori_loop(1, n, finish, total)
+        origin = (chip + half - k) % half
+        remote(
+            DOWN, dpair.at[origin], drecv.at[origin], 0, origin, 2 * origin + core
+        ).wait_recv()
+        return total + drecv[origin].astype(f32)
+
+    total = lax.fori_loop(1, half, finish, total)
     out[...] = total.astype(bf16)
-    loop(1, n, functools.partial(sent_one, DOWN, dsend, drecv))
+    loop(0, half, lambda i: to_pair((chip + 1 + i) % half, i).wait_send())
+    loop(1, half, lambda k: to_chip(k).wait_send())
 
 
 def body(*args):
@@ -676,7 +699,7 @@
         + [
             exchange,
             exchange,
-            pltpu.VMEM((KV_HEADS, samples * GROUP, LANES), f32),
+            pltpu.VMEM((KV_HEADS, samples, GROUP, LANES), bf16),
             parts,
             parts,
             stats,
@@ -685,9 +708,9 @@
             fresh,
             parts,
             exchange,
-            exchange,
-            exchange,
-            exchange,
+            pltpu.VMEM((n // 2, samples, width), bf16),
+            pltpu.VMEM((n // 2, samples, width), bf16),
+            pltpu.VMEM((n // 2, samples, width), bf16),
             pltpu.SemaphoreType.DMA((9,)),
             pltpu.SemaphoreType.DMA((5, n)),
             pltpu.SemaphoreType.DMA((PHASES, n)),

time: 70.2 us -> 64.1 us (0.913)
  Pallas kernels: 68.3 us -> 62.4 us
    pallas_call x1, Pallas kernels: 68.3 us -> 62.4 us  [body(): pl.pallas_call(functools.partial(layer_kernel, n, prefix_keys.shape[0] *...]
where the time goes in v2:
time: 64.1 us; the launch traced here: 63.8 us
  Pallas kernels  62.4 us (97%)
  local copies, waits for them, and re-layouts  1.32 us (2%)
    pallas_call x1, Pallas kernels, body(): pl.pallas_call(functools.partial(layer_kernel, n, prefix_keys.shape[0] *...  62.4 us
    unnamed x1, local copies, waits for them, and re-layouts  1.32 us

profile of v2, /device:TPU:0, one launch (start us, length us, event | category | flops | bytes accessed | tf_op | source)
XLA Modules:
  0.0 63.8 jit_solution(7173782773112594975)
XLA Ops:
  0.0 62.4 %layer.1 = bf16[16,512]{1,0:T(8,128)(2,1)} custom-call(bf16[16,512]{1,0:T(8,128)(2,1)} %tokens.1, f32[1,8192]{1,0:T(1,128)} %bitcast.2, f32[1,8192]{1,0:T(1,128)} %bitcast.3, bf16[8192,512]{1,0:T(8,128)(2,1)} %q_hbm.1, bf16[512,1024]{1,0:T(8,128)(2,1)} %k_hbm.1, bf16[512,1024]{1,0:T(8,128)(2,1)} %v_hbm.1, bf16[8192,512]{1,0:T(8,128)(2,1)} %o_hbm.1, ...), custom_call_target="tpu_custom_call" | custom-call | tf_op jit(solution)/shard_map/layer/pallas_call | solution.py:690
  62.4 1.3 %copy.18 = bf16[16,512]{1,0:T(8,128)(2,1)} copy(bf16[16,512]{1,0:T(8,128)(2,1)} %layer.1) | data formatting | bytes 32768

commit v3 on v2

--- a/solution.py
+++ b/solution.py
@@ -295,18 +295,20 @@
         )
         remote(phase, buf.at[me], buf.at[me], 0, me, partner).start()
 
+    def relay(phase, buf, k):
+        origin = (me + n - 2 * k) % n
+        remote(phase, buf.at[origin], buf.at[origin], 0, origin, partner).wait_recv()
+        remote(phase, buf.at[origin], buf.at[origin], half + k, origin, partner).start()
+        return origin
+
+    def arrive(phase, buf, k):
+        origin = (partner + n - 2 * k) % n
+        remote(phase, buf.at[origin], buf.at[origin], 0, origin, partner).wait_recv()
+        return origin
+
     def collect(phase, buf):
-        def relay(k):
-            origin = (me + n - 2 * k) % n
-            remote(phase, buf.at[origin], buf.at[origin], 0, origin, partner).wait_recv()
-            remote(phase, buf.at[origin], buf.at[origin], half + k, origin, partner).start()
-
-        def arrive(k):
-            origin = (partner + n - 2 * k) % n
-            remote(phase, buf.at[origin], buf.at[origin], 0, origin, partner).wait_recv()
-
-        loop(1, half, relay)
-        loop(0, half, arrive)
+        loop(1, half, functools.partial(relay, phase, buf))
+        loop(0, half, functools.partial(arrive, phase, buf))
 
     def drain(phase, buf):
         def one(k):
@@ -585,20 +587,28 @@
     attended = lax.fori_loop(0, n, o_step, jnp.zeros((samples, width), f32), unroll=4)
     mixbuf[me] = (tokbuf[me].astype(f32) + attended).astype(bf16)
     spread(MIX, mixbuf)
-    collect(MIX, mixbuf)
-    root = inverse_root(mixbuf)
 
     def ffn_step(d, carry):
-        gate, up = carry
+        gate, up, squares = carry
         chunk(2, d).wait()
         chunk(3, d).wait()
-        part = normed(mixbuf, root, mgain, d)
+        block = mixbuf[d].astype(f32)
+        part = (block * mgain[:, rows_of(d)]).astype(bf16)
         gate = gate + jnp.dot(part, gw[rows_of(d), :], preferred_element_type=f32)
         up = up + jnp.dot(part, uw[rows_of(d), :], preferred_element_type=f32)
-        return gate, up
+        return gate, up, squares + jnp.sum(block * block, axis=1, keepdims=True)
 
     zero = jnp.zeros((samples, ffn), f32)
-    gate, up = lax.fori_loop(0, n, ffn_step, (zero, zero), unroll=4)
+    carry = ffn_step(me, (zero, zero, jnp.zeros((samples, 1), f32)))
+    carry = lax.fori_loop(
+        1, half, lambda k, c: ffn_step(relay(MIX, mixbuf, k), c), carry
+    )
+    gate, up, squares = lax.fori_loop(
+        0, half, lambda k, c: ffn_step(arrive(MIX, mixbuf, k), c), carry, unroll=4
+    )
+    root = lax.rsqrt(squares / (n * width) + EPSILON)
+    gate = gate * root
+    up = up * root
     hidden = (gate / (1.0 + jnp.exp(-gate)) * up).astype(bf16)
 
     def down_step(step, weights, place):

time: 64.1 us -> 61.9 us (0.966)
  Pallas kernels: 62.4 us -> 60.2 us
    pallas_call x1, Pallas kernels: 62.4 us -> 60.2 us  [body(): pl.pallas_call(functools.partial(layer_kernel, n, prefix_keys.shape[0] *...]
where the time goes in v3:
time: 61.9 us; the launch traced here: 61.5 us
  Pallas kernels  60.2 us (97%)
  local copies, waits for them, and re-layouts  1.32 us (2%)
    pallas_call x1, Pallas kernels, body(): pl.pallas_call(functools.partial(layer_kernel, n, prefix_keys.shape[0] *...  60.2 us
    unnamed x1, local copies, waits for them, and re-layouts  1.32 us

profile of v3, /device:TPU:0, one launch (start us, length us, event | category | flops | bytes accessed | tf_op | source)
XLA Modules:
  0.0 61.5 jit_solution(17837883395486749495)
XLA Ops:
  0.0 60.2 %layer.1 = bf16[16,512]{1,0:T(8,128)(2,1)} custom-call(bf16[16,512]{1,0:T(8,128)(2,1)} %tokens.1, f32[1,8192]{1,0:T(1,128)} %bitcast.2, f32[1,8192]{1,0:T(1,128)} %bitcast.3, bf16[8192,512]{1,0:T(8,128)(2,1)} %q_hbm.1, bf16[512,1024]{1,0:T(8,128)(2,1)} %k_hbm.1, bf16[512,1024]{1,0:T(8,128)(2,1)} %v_hbm.1, bf16[8192,512]{1,0:T(8,128)(2,1)} %o_hbm.1, ...), custom_call_target="tpu_custom_call" | custom-call | tf_op jit(solution)/shard_map/layer/pallas_call | solution.py:700
  60.2 1.3 %copy.18 = bf16[16,512]{1,0:T(8,128)(2,1)} copy(bf16[16,512]{1,0:T(8,128)(2,1)} %layer.1) | data formatting | bytes 32768
